TPU v7x, 32 devices: a whole 2x2x4 slice. The times are simulated.
32 devices in a mesh: shot: 4 (over y, x), tile: 8 (over z, core).
Axes of the slice: x: 2, y: 2, z: 4, core: 2. Of those that a mesh axis runs over, the one named last changes fastest.
Arguments:
- p_now: float32 [4, 1024, 16, 128], P('shot', 'tile'), may hold values from -6 to 6
- p_prev: float32 [4, 1024, 16, 128], P('shot', 'tile'), may hold values from -6 to 6
- adj_now: float32 [4, 1024, 16, 128], P('shot', 'tile'), may hold values from -60 to 60
- adj_next: float32 [4, 1024, 16, 128], P('shot', 'tile'), may hold values from -60 to 60
- coef_old: float32 [512, 512], P('tile'), may hold values from 0.14 to 0.28
- signs: int32 [4, 512], P('shot', 'tile'), may hold values from 0 to 1
- elem_index: int32 [512], P('tile'), may hold values from 0 to 262143
- wavelet: float32 [5], replicated, may hold values from -4 to 4
Outputs:
- direction: float32 [512, 512], P('tile')
- p_last: float32 [4, 1024, 16, 128], P('shot', 'tile')
All inputs are finite; a program needn't handle non-finite values.
Results may differ from a plain program's by a relative error of at most 0.0003.
Values sent between devices are 32-bit elements; how exact they have to be, the bound alone decides.
A program may use at most 64 MiB of HBM per device.

v0:
```python
import functools

import jax
import jax.numpy as jnp
import ml_dtypes
import numpy as np
from jax import lax
from jax.experimental import pallas as pl
from jax.experimental.pallas import tpu as pltpu
from jax.sharding import PartitionSpec as P

OV = 8
LEARN = 0.02
EPSILON = 1e-06
F32 = jnp.float32
BF16 = jnp.bfloat16
MESH = pl.DeviceIdType.MESH


def spectral_second(length):
    index = np.arange(length)
    number = np.minimum(index, length - index) * (2.0 * np.pi / length)
    gap = (index[:, None] - index[None, :])[:, :, None] * index[None, None, :] % length
    return np.sum(-(number * number) / length * np.cos(2.0 * np.pi / length * gap), axis=-1)


def spline_weight(offset):
    mag = np.abs(offset)
    inner = 2.0 / 3.0 - mag * mag + 0.5 * mag * mag * mag
    outer = (2.0 - mag) ** 3 / 6.0
    return np.where(mag < 1.0, inner, np.where(mag < 2.0, outer, 0.0))


def periodic_spline(fine, coarse):
    gap = np.arange(fine)[:, None] - 2 * np.arange(coarse)[None, :]
    return sum(spline_weight((gap + image * fine - 0.5) * 0.5) for image in range(-2, 3))


def halves(matrix):
    high = matrix.astype(np.float32).astype(ml_dtypes.bfloat16)
    low = (matrix - high.astype(np.float64)).astype(ml_dtypes.bfloat16)
    return high, low


def twice(block):
    out = np.zeros((2 * block.shape[0], 2 * block.shape[1]))
    out[: block.shape[0], : block.shape[1]] = block
    out[block.shape[0] :, block.shape[1] :] = block
    return out


def constants(cx, cz, cxc, czc):
    full = cx + 2 * OV
    ramp = np.sin(0.5 * np.pi * (np.arange(OV) + 0.5) / OV) ** 2
    second_x = spectral_second(full)[OV : OV + cx]
    high, low = halves(second_x[:, OV : OV + cx])
    core_x = np.block([[high, high], [low, low]])
    rim = np.concatenate([second_x[:, :OV] * ramp, second_x[:, OV + cx :] * ramp[::-1]], 1)
    high, low = halves(rim)
    rim_x = np.block([[high, high], [low, low]])
    high, low = halves(spectral_second(cz))
    core_z = np.block([[high, low], [high, low]])
    gap = np.arange(cx)[:, None] - 2 * (np.arange(cxc + 2 * OV)[None, :] - OV)
    expand_x = spline_weight((gap - 0.5) * 0.5)
    spline_z = periodic_spline(cz, czc)
    floats = [expand_x, twice(spline_z.T), expand_x.T, twice(spline_z)]
    return [core_x, rim_x, core_z] + [m.astype(np.float32) for m in floats]


def split(value):
    high = value.astype(BF16)
    return high, (value - high.astype(F32)).astype(BF16)


def dot(a, b):
    return jnp.dot(a, b, preferred_element_type=F32)


def dot3(a, b):
    ah, al = split(a)
    bh, bl = split(b)
    return dot(ah, bh) + (dot(ah, bl) + dot(al, bh))


def kernel(
    dims, n_shot, n_tile, spline_y,
    p_now, p_prev, q_now, q_next, coef_in, signs, elems, wave,
    core_x_in, rim_x_in, core_z_in, exp_x_in, exp_z_in, pro_x_in, pro_z_in,
    direction, p_last,
    raw, raw_sem, pf, qf, lp, lq, sig, sig2, src, wide, exp_t,
    ph, qh, cext, narrow, part0, rims, part, rs, tot, ttot, sq_out, sq_in,
    ph_s, ph_r, qh_s, qh_r, ce_s, ce_r, ri_s, ri_r, rs_s, rs_r, ag_s, ag_r, sq_s, sq_r,
    sq_all, sa_s, sa_r, consts_sem, coef, core_x, rim_x, core_z, exp_x, exp_z, pro_x, pro_z,
):
    cx, cy, cz, cxc, pairs, steps, group, rows = dims
    shot = lax.axis_index("shot")
    tile = lax.axis_index("tile")
    has_left = tile > 0
    has_right = tile < n_tile - 1
    ext = cxc + 2 * OV

    barrier = pltpu.get_barrier_semaphore()
    for d in range(1, n_tile):
        pl.semaphore_signal(
            barrier, inc=1, device_id={"tile": lax.rem(tile + d, n_tile)}, device_id_type=MESH
        )
    for d in range(1, n_shot):
        pl.semaphore_signal(
            barrier, inc=1, device_id={"shot": lax.rem(shot + d, n_shot)}, device_id_type=MESH
        )

    def load(ref, out, s):
        copy = pltpu.make_async_copy(ref, out, s)
        copy.start()
        return copy

    fields = (p_now, q_now, p_prev, q_next)
    matrices = (
        (core_x_in, core_x), (core_z_in, core_z), (rim_x_in, rim_x), (exp_x_in, exp_x),
        (exp_z_in, exp_z), (pro_x_in, pro_x), (pro_z_in, pro_z),
    )
    loads = [load(fields[0], raw.at[0], raw_sem.at[0])]
    coef_load = load(coef_in, coef, consts_sem.at[0])
    loads.append(load(fields[1], raw.at[1], raw_sem.at[1]))
    matrix_loads = [load(a, b, consts_sem.at[i + 1]) for i, (a, b) in enumerate(matrices)]
    loads += [load(fields[i], raw.at[i], raw_sem.at[i]) for i in (2, 3)]

    def to_planes(i, out):
        loads[i].wait()
        for y in range(cy):
            out[y] = raw[i, pl.ds(y, cx, stride=cy), :]

    @pl.when(jnp.logical_not(has_left))
    def _():
        ph[:, 0] = jnp.zeros_like(ph[:, 0])
        qh[:, 0] = jnp.zeros_like(qh[:, 0])
        cext[:, :OV, :] = jnp.zeros((pairs, OV, 128), F32)
        rims[0] = jnp.zeros_like(rims[0])

    @pl.when(jnp.logical_not(has_right))
    def _():
        ph[:, 1] = jnp.zeros_like(ph[:, 1])
        qh[:, 1] = jnp.zeros_like(qh[:, 1])
        cext[:, OV + cxc :, :] = jnp.zeros((pairs, OV, 128), F32)
        rims[1] = jnp.zeros_like(rims[1])

    def beside(to_right, right_dst, to_left, left_dst, ss, rr):
        right = pltpu.make_async_remote_copy(
            src_ref=to_right, dst_ref=right_dst, send_sem=ss.at[0], recv_sem=rr.at[0],
            device_id={"tile": lax.rem(tile + 1, n_tile)}, device_id_type=MESH,
        )
        left = pltpu.make_async_remote_copy(
            src_ref=to_left, dst_ref=left_dst, send_sem=ss.at[1], recv_sem=rr.at[1],
            device_id={"tile": lax.rem(tile + n_tile - 1, n_tile)}, device_id_type=MESH,
        )
        return right, left

    def start(pair):
        @pl.when(has_right)
        def _():
            pair[0].start()

        @pl.when(has_left)
        def _():
            pair[1].start()

    def finish(pair):
        @pl.when(has_right)
        def _():
            pair[0].wait_send()
            pair[1].wait_recv()

        @pl.when(has_left)
        def _():
            pair[1].wait_send()
            pair[0].wait_recv()

    def field_halo(field, index, halo, t, ss, rr):
        return beside(
            field.at[index, :, cx - OV :, :], halo.at[t, 0],
            field.at[index, :, :OV, :], halo.at[t, 1], ss.at[t], rr.at[t],
        )

    p_halo = lambda t: field_halo(pf, t + 1, ph, t, ph_s, ph_r)
    q_halo = lambda t: field_halo(qf, t + 1, qh, t, qh_s, qh_r)

    to_planes(0, pf.at[1])
    pl.semaphore_wait(barrier, n_tile + n_shot - 2)
    start(p_halo(0))
    to_planes(1, qf.at[1])
    start(q_halo(0))
    coef_load.wait()
    for a in range(pairs):
        cext[a, OV : OV + cxc, :] = coef[:, a * 128 : (a + 1) * 128]
    coef_rims = beside(
        cext.at[:, cxc : cxc + OV, :], cext.at[:, :OV, :],
        cext.at[:, OV : 2 * OV, :], cext.at[:, OV + cxc :, :], ce_s, ce_r,
    )
    start(coef_rims)

    def core(field, out):
        def body(i, carry):
            y0 = 2 * i
            y1 = y0 + 1
            a = field[y0]
            b = field[y1]
            high, low = split(jnp.concatenate([a, b], 1))
            ox = dot(core_x[...], jnp.concatenate([high, low], 0))
            oz = dot(
                jnp.concatenate(
                    [
                        jnp.concatenate([high[:, :cz], low[:, :cz]], 1),
                        jnp.concatenate([high[:, cz:], low[:, cz:]], 1),
                    ],
                    0,
                ),
                core_z[...],
            )
            before = field[lax.rem(y0 + cy - 1, cy)]
            after = field[lax.rem(y1 + 1, cy)]
            ox = ox[:cx] + ox[cx:]
            oz = oz[:, :cz] + oz[:, cz:]
            out[y0] = ox[:, :cz] + (before + b - 2.0 * a) + oz[:cx]
            out[y1] = ox[:, cz:] + (a + after - 2.0 * b) + oz[cx:]
            return carry

        lax.fori_loop(0, cy // 2, body, 0, unroll=2)

    def with_rim(halo, lap, use, out, keep):
        def body(i, carry):
            y0 = 2 * i
            y1 = y0 + 1
            edge = jnp.concatenate(
                [
                    jnp.concatenate([halo[0, y0], halo[0, y1]], 1),
                    jnp.concatenate([halo[1, y0], halo[1, y1]], 1),
                ],
                0,
            )
            ox = dot(rim_x[...], jnp.concatenate(split(edge), 0))
            ox = ox[:cx] + ox[cx:]
            laps = (lap[y0] + ox[:, :cz], lap[y1] + ox[:, cz:])
            nexts = [use(y, value) for y, value in zip((y0, y1), laps)]
            for y, value, new in zip((y0, y1), laps, nexts):
                if keep is not None:
                    keep[y] = value
                if new is not None:
                    out[y] = new
            return carry

        lax.fori_loop(0, cy // 2, body, 0, unroll=2)

    def expand(coefs, out):
        for a in range(pairs):
            both = dot3(dot3(exp_x[...], coefs[a]), exp_z[...])
            wide[2 * a] = both[:, :cz]
            wide[2 * a + 1] = both[:, cz:]

        def body(i, carry):
            at = pl.ds(pl.multiple_of(i * 8, 8), 8)
            planes = [wide[j, at, :] for j in range(2 * pairs)]
            for y in range(cy):
                terms = [
                    float(spline_y[y, j]) * planes[j] for j in range(2 * pairs) if spline_y[y, j] != 0
                ]
                out[y, at, :] = functools.reduce(lambda u, v: u + v, terms)
            return carry

        lax.fori_loop(0, cx // 8, body, 0)

    count = elems.shape[1]
    where_to = elems[...]
    amount = (2 * signs[...] - 1).astype(F32)
    row_of = lax.rem(lax.div(where_to, cz), cy) * cx + lax.div(where_to, cz * cy)
    lanes = (lax.broadcasted_iota(jnp.int32, (cz, count), 0) == lax.rem(where_to, cz)).astype(F32)
    lanes = lanes.astype(BF16)

    def source(y, carry):
        place = lax.broadcasted_iota(jnp.int32, (cx, count), 0) + y * cx
        hits = jnp.where(place == row_of, amount, 0.0).astype(BF16)
        src[y] = lax.dot_general(hits, lanes, (((1,), (1,)), ((), ())), preferred_element_type=F32)
        return carry

    lax.fori_loop(0, cy, source, 0, unroll=2)
    to_planes(2, pf.at[0])
    to_planes(3, qf.at[0])
    for copy in matrix_loads:
        copy.wait()
    finish(coef_rims)
    expand(cext, sig)

    def square(y, carry):
        value = sig[y]
        sig2[y] = value * value
        return carry

    lax.fori_loop(0, cy, square, 0)

    def step(t, carry):
        core(pf.at[t + 1], lp.at[t])
        core(qf.at[t + 1], lq)
        finish(p_halo(t))
        scale = wave[t]

        def use_p(y, lap):
            return 2.0 * pf[t + 1, y] - pf[t, y] + sig2[y] * lap + scale * src[y]

        with_rim(ph.at[t], lp.at[t], use_p, pf.at[t + 2], lp.at[t])
        start(p_halo(t + 1))
        finish(q_halo(t))

        def use_q(y, lap):
            return 2.0 * qf[t + 1, y] - qf[t, y] + sig2[y] * lap

        with_rim(qh.at[t], lq, use_q, qf.at[t + 2], None)

        @pl.when(t < steps - 1)
        def _():
            start(q_halo(t + 1))

        return carry

    lax.fori_loop(0, steps, step, 0)

    def image(i, carry):
        at = pl.ds(pl.multiple_of(i * 8, 8), 8)
        out = [None] * (2 * pairs)
        for y in range(cy):
            summed = qf[steps + 1, y, at, :] * lp[0, y, at, :]
            for t in range(1, steps):
                summed = summed + qf[steps + 1 - t, y, at, :] * lp[t, y, at, :]
            value = 2.0 * sig[y, at, :] * summed
            for j in range(2 * pairs):
                if spline_y[y, j] != 0:
                    term = float(spline_y[y, j]) * value
                    out[j] = term if out[j] is None else out[j] + term
        for j in range(2 * pairs):
            narrow[j, at, :] = out[j]
        return carry

    lax.fori_loop(0, cx // 8, image, 0)
    for a in range(pairs):
        both = jnp.concatenate([narrow[2 * a], narrow[2 * a + 1]], 1)
        part0[a] = dot3(dot3(pro_x[...], both), pro_z[...])
    part_rims = beside(
        part0.at[:, cxc:, :], rims.at[0], part0.at[:, : 2 * OV, :], rims.at[1], ri_s, ri_r
    )
    start(part_rims)
    core(pf.at[steps + 1], lp.at[steps])
    finish(part_rims)
    halfs = ext // rows
    for a in range(pairs):
        whole = jnp.concatenate(
            [
                part0[a, : 2 * OV, :] + rims[0, a],
                part0[a, 2 * OV : cxc, :],
                part0[a, cxc:, :] + rims[1, a],
            ],
            0,
        )
        for r in range(halfs):
            flat = a * halfs + r
            part[flat // group, flat % group] = whole[r * rows : (r + 1) * rows]

    def peer_copy(source_ref, target_ref, d, ss, rr):
        return pltpu.make_async_remote_copy(
            src_ref=source_ref, dst_ref=target_ref, send_sem=ss.at[d - 1], recv_sem=rr.at[d - 1],
            device_id={"shot": lax.rem(shot + d, n_shot)}, device_id_type=MESH,
        )

    scatter = []
    for d in range(1, n_shot):
        copy = peer_copy(part.at[lax.rem(shot + d, n_shot)], rs.at[d - 1], d, rs_s, rs_r)
        copy.start()
        scatter.append(copy)
    finish(p_halo(steps))

    with_rim(ph.at[steps], lp.at[steps], lambda y, lap: None, None, lp.at[steps])
    mine = part[shot]
    for d in range(1, n_shot):
        scatter[d - 1].wait()
        mine = mine + rs[d - 1]
    tot[shot] = mine
    gather = []
    for d in range(1, n_shot):
        copy = peer_copy(tot.at[shot], tot.at[shot], d, ag_s, ag_r)
        copy.start()
        gather.append(copy)
    squares = jnp.zeros((8, 128), F32)
    first = lax.rem(shot, halfs) * rows
    for g in range(group):
        for r in range(0, rows, 8):
            inside = jnp.logical_and(first + r >= OV, first + r < OV + cxc)
            value = mine[g, r : r + 8] * jnp.where(inside, 1.0, 0.0).astype(F32)
            squares = squares + value * mine[g, r : r + 8]
    sq_out[...] = squares
    sums = []
    for d in range(1, n_tile):
        copy = pltpu.make_async_remote_copy(
            src_ref=sq_out, dst_ref=sq_in.at[d - 1], send_sem=sq_s.at[d - 1], recv_sem=sq_r.at[d - 1],
            device_id={"tile": lax.rem(tile + d, n_tile)}, device_id_type=MESH,
        )
        copy.start()
        sums.append(copy)
    for d in range(1, n_tile):
        sums[d - 1].wait()
        squares = squares + sq_in[d - 1]
    sq_all[shot] = squares
    sums = []
    for d in range(1, n_shot):
        copy = peer_copy(sq_all.at[shot], sq_all.at[shot], d, sa_s, sa_r)
        copy.start()
        sums.append(copy)
    for copy in gather:
        copy.wait()
    left_on = jnp.where(has_left, 1.0, 0.0).astype(F32)
    right_on = jnp.where(has_right, 1.0, 0.0).astype(F32)
    for a in range(pairs):
        pieces = []
        for r in range(halfs):
            flat = a * halfs + r
            pieces.append(tot[flat // group, flat % group])
        whole = pieces[0] if halfs == 1 else jnp.concatenate(pieces, 0)
        ttot[a, :OV, :] = whole[:OV] * left_on
        ttot[a, OV : OV + cxc, :] = whole[OV : OV + cxc]
        ttot[a, OV + cxc :, :] = whole[OV + cxc :] * right_on
    expand(ttot, exp_t)
    for copy in sums:
        copy.wait()
    squares = sq_all[0]
    for d in range(1, n_shot):
        squares = squares + sq_all[d]
    cells = float(n_tile * cxc * 2 * pairs * 64)
    mean = jnp.sum(jnp.sum(squares, axis=0, keepdims=True), axis=1, keepdims=True) / cells
    scale = 1.0 / jnp.sqrt(mean + EPSILON)
    for a in range(pairs):
        direction[:, a * 128 : (a + 1) * 128] = ttot[a, OV : OV + cxc, :] * scale
    moved = LEARN * scale
    last = wave[steps]
    for y in range(cy):
        speed = sig[y] - moved * exp_t[y]
        p_last[pl.ds(y, cx, stride=cy), :] = (
            2.0 * pf[steps + 1, y] - pf[steps, y] + speed * speed * lp[steps, y] + last * src[y]
        )


def on_device(n_shot, n_tile, p_now, p_prev, adj_now, adj_next, coef_old, signs, elem_index, wavelet):
    _, cx, cy, cz = p_now.shape
    cxc, merged = coef_old.shape
    steps = wavelet.shape[0] - 1
    cyc = cy // 2
    czc = merged // cyc
    pairs = cyc // 2
    spline_y = periodic_spline(cy, cyc).astype(np.float32)
    ext = cxc + 2 * OV
    group = max(1, pairs // n_shot)
    rows = ext // max(1, n_shot // pairs)
    dims = (cx, cy, cz, cxc, pairs, steps, group, rows)
    flat = lambda v: v.reshape(cx * cy, cz)
    consts = [jnp.asarray(c) for c in constants(cx, cz, cxc, czc)]
    vmem = pl.BlockSpec(memory_space=pltpu.VMEM)
    held = lambda v: pltpu.with_memory_space_constraint(v, pltpu.HBM)
    field = (cy, cx, cz)
    buf = lambda *shape: pltpu.VMEM(shape, F32)
    sem = lambda *shape: pltpu.SemaphoreType.DMA(shape)
    direction, p_last = pl.pallas_call(
        functools.partial(kernel, dims, n_shot, n_tile, spline_y),
        out_shape=(
            jax.ShapeDtypeStruct((cxc, merged), F32),
            jax.ShapeDtypeStruct((cx * cy, cz), F32),
        ),
        in_specs=[pl.BlockSpec(memory_space=pltpu.HBM)] * 5
        + [vmem] * 2
        + [pl.BlockSpec(memory_space=pltpu.SMEM)]
        + [pl.BlockSpec(memory_space=pltpu.HBM)] * len(consts),
        out_specs=(vmem, vmem),
        scratch_shapes=[
            buf(4, cx * cy, cz), sem(4),
            buf(steps + 2, *field), buf(steps + 2, *field), buf(steps + 1, *field), buf(*field),
            buf(*field), buf(*field), buf(*field), buf(cyc, cx, cz), buf(*field),
            buf(steps + 1, 2, cy, OV, cz), buf(steps, 2, cy, OV, cz),
            buf(pairs, ext, 128), buf(cyc, cx, cz), buf(pairs, ext, 128),
            buf(2, pairs, 2 * OV, 128),
            buf(n_shot, group, rows, 128), buf(max(1, n_shot - 1), group, rows, 128),
            buf(n_shot, group, rows, 128), buf(pairs, ext, 128),
            buf(8, 128), buf(max(1, n_tile - 1), 8, 128),
            sem(steps + 1, 2), sem(steps + 1, 2), sem(steps, 2), sem(steps, 2),
            sem(2), sem(2), sem(2), sem(2),
            sem(max(1, n_shot - 1)), sem(max(1, n_shot - 1)),
            sem(max(1, n_shot - 1)), sem(max(1, n_shot - 1)),
            sem(max(1, n_tile - 1)), sem(max(1, n_tile - 1)),
            buf(n_shot, 8, 128), sem(max(1, n_shot - 1)), sem(max(1, n_shot - 1)),
            sem(1 + len(consts)), buf(cxc, merged),
        ]
        + [pltpu.VMEM(c.shape, c.dtype) for c in consts],
        compiler_params=pltpu.CompilerParams(
            collective_id=0, has_side_effects=True, vmem_limit_bytes=38 * 1024 * 1024
        ),
    )(
        *map(held, (flat(p_now), flat(p_prev), flat(adj_now), flat(adj_next), coef_old)),
        signs, elem_index.reshape(1, -1), wavelet, *map(held, consts),
    )
    return direction, p_last.reshape(1, cx, cy, cz)


def solution(mesh):
    placed = (
        P("shot", "tile", None, None),
        P("shot", "tile", None, None),
        P("shot", "tile", None, None),
        P("shot", "tile", None, None),
        P("tile", None),
        P("shot", "tile"),
        P("tile"),
        P(),
    )
    return jax.shard_map(
        functools.partial(on_device, mesh.shape["shot"], mesh.shape["tile"]),
        mesh=mesh,
        in_specs=placed,
        out_specs=(P("tile", None), P("shot", "tile", None, None)),
        check_vma=False,
    )
```

profile of v0, /device:TPU:0, one launch (start us, length us, event | category | flops | bytes accessed | tf_op | source)
XLA Modules:
  0.0 48.6 jit_solution(2001029674451837499)
XLA Ops:
  0.6 0.0 copy-start
  0.6 0.0 copy-start.1
  0.7 0.0 copy-start.2
  0.7 0.6 %copy-done = s32[1,64]{1,0:T(1,128)S(1)} copy-done((s32[1,64]{1,0:T(1,128)S(1)}, s32[1,64]{1,0:T(1,128)}, u32[]{:S(2)}) %copy-start) | copy-done | bytes 280
  1.3 0.0 copy-done.1
  1.3 0.0 copy-done.2
  1.3 45.7 %shard_map.158 = (f32[64,512]{1,0:T(8,128)S(1)}, f32[2048,128]{1,0:T(8,128)S(1)}) custom-call(f32[2048,128]{1,0:T(8,128)} %bitcast.8, f32[2048,128]{1,0:T(8,128)} %bitcast.9, f32[2048,128]{1,0:T(8,128)} %bitcast.10, f32[2048,128]{1,0:T(8,128)} %bitcast.11, f32[64,512]{1,0:T(8,128)} %coef_in.1, s32[1,64]{1,0:T(1,128)S(1)} %copy-done, s32[1,64]{1,0:T(1,128)S(1)} %bitcast.7, ...), custom_call_target="tpu_custom_call" | custom-call | tf_op jit(solution)/shard_map/pallas_call | solution.py:466
  47.0 0.7 %copy.19 = f32[64,512]{1,0:T(8,128)} copy(f32[64,512]{1,0:T(8,128)S(1)} %get-tuple-element.8) | data formatting | bytes 262144
  47.7 1.0 %copy.20 = f32[1,128,16,128]{3,2,1,0:T(8,128)} copy(f32[1,128,16,128]{3,2,1,0:T(8,128)S(1)} %bitcast.6) | data formatting | bytes 2097152
Async XLA Ops:
  0.6 0.7 %copy-start = (s32[1,64]{1,0:T(1,128)S(1)}, s32[1,64]{1,0:T(1,128)}, u32[]{:S(2)}) copy-start(s32[1,64]{1,0:T(1,128)} %signs.1) | copy-start | bytes 772
  0.6 0.7 %copy-start.1 = (s32[64]{0:T(128)S(1)}, s32[64]{0:T(128)}, u32[]{:S(2)}) copy-start(s32[64]{0:T(128)} %param.21) | copy-start | bytes 772
  0.7 0.7 %copy-start.2 = (f32[5]{0:T(128)S(1)}, f32[5]{0:T(128)}, u32[]{:S(2)}) copy-start(f32[5]{0:T(128)} %wave.1) | copy-start | bytes 64
where the time goes:
time: 48.8 us; the launch traced here: 48.6 us
  Pallas kernels  45.7 us (94%)
  local copies, waits for them, and re-layouts  2.29 us (5%)
  between operations  0.67 us (1%)
    pallas_call x1, Pallas kernels, on_device(): pl.pallas_call(functools.partial(kernel, dims, n_shot, n_tile, spline_y),...  45.7 us
    unnamed x8, local copies, waits for them, and re-layouts  2.29 us

commit v1 on v0

--- a/solution.py
+++ b/solution.py
@@ -53,18 +53,17 @@
     full = cx + 2 * OV
     ramp = np.sin(0.5 * np.pi * (np.arange(OV) + 0.5) / OV) ** 2
     second_x = spectral_second(full)[OV : OV + cx]
-    high, low = halves(second_x[:, OV : OV + cx])
-    core_x = np.block([[high, high], [low, low]])
+    high, low = halves(second_x[:, OV : OV + cx] - 2.0 * np.eye(cx))
     rim = np.concatenate([second_x[:, :OV] * ramp, second_x[:, OV + cx :] * ramp[::-1]], 1)
-    high, low = halves(rim)
-    rim_x = np.block([[high, high], [low, low]])
+    rim_high, rim_low = halves(rim)
+    core_x = np.concatenate([high, high, low, rim_high, rim_high, rim_low, rim_low], 1)
     high, low = halves(spectral_second(cz))
     core_z = np.block([[high, low], [high, low]])
     gap = np.arange(cx)[:, None] - 2 * (np.arange(cxc + 2 * OV)[None, :] - OV)
     expand_x = spline_weight((gap - 0.5) * 0.5)
     spline_z = periodic_spline(cz, czc)
     floats = [expand_x, twice(spline_z.T), expand_x.T, twice(spline_z)]
-    return [core_x, rim_x, core_z] + [m.astype(np.float32) for m in floats]
+    return [core_x, core_z] + [m.astype(np.float32) for m in floats]
 
 
 def split(value):
@@ -85,12 +84,12 @@
 def kernel(
     dims, n_shot, n_tile, spline_y,
     p_now, p_prev, q_now, q_next, coef_in, signs, elems, wave,
-    core_x_in, rim_x_in, core_z_in, exp_x_in, exp_z_in, pro_x_in, pro_z_in,
+    core_x_in, core_z_in, exp_x_in, exp_z_in, pro_x_in, pro_z_in,
     direction, p_last,
-    raw, raw_sem, pf, qf, lp, lq, sig, sig2, src, wide, exp_t,
+    raw, raw_sem, pf, qf, lp, dp, dq, sig, sig2, src, wide, exp_t,
     ph, qh, cext, narrow, part0, rims, part, rs, tot, ttot, sq_out, sq_in,
     ph_s, ph_r, qh_s, qh_r, ce_s, ce_r, ri_s, ri_r, rs_s, rs_r, ag_s, ag_r, sq_s, sq_r,
-    sq_all, sa_s, sa_r, consts_sem, coef, core_x, rim_x, core_z, exp_x, exp_z, pro_x, pro_z,
+    sq_all, sa_s, sa_r, consts_sem, coef, core_x, core_z, exp_x, exp_z, pro_x, pro_z,
 ):
     cx, cy, cz, cxc, pairs, steps, group, rows = dims
     shot = lax.axis_index("shot")
@@ -116,7 +115,7 @@
 
     fields = (p_now, q_now, p_prev, q_next)
     matrices = (
-        (core_x_in, core_x), (core_z_in, core_z), (rim_x_in, rim_x), (exp_x_in, exp_x),
+        (core_x_in, core_x), (core_z_in, core_z), (exp_x_in, exp_x),
         (exp_z_in, exp_z), (pro_x_in, pro_x), (pro_z_in, pro_z),
     )
     loads = [load(fields[0], raw.at[0], raw_sem.at[0])]
@@ -129,6 +128,11 @@
         loads[i].wait()
         for y in range(cy):
             out[y] = raw[i, pl.ds(y, cx, stride=cy), :]
+
+    def to_steps(i, now, out):
+        loads[i].wait()
+        for y in range(cy):
+            out[y] = now[y] - raw[i, pl.ds(y, cx, stride=cy), :]
 
     @pl.when(jnp.logical_not(has_left))
     def _():
@@ -198,14 +202,21 @@
     )
     start(coef_rims)
 
-    def core(field, out):
-        def body(i, carry):
-            y0 = 2 * i
-            y1 = y0 + 1
+    def laplace(field, halo, use):
+        for i in range(cy // 2):
+            y0, y1 = 2 * i, 2 * i + 1
             a = field[y0]
             b = field[y1]
             high, low = split(jnp.concatenate([a, b], 1))
-            ox = dot(core_x[...], jnp.concatenate([high, low], 0))
+            edge = jnp.concatenate(
+                [
+                    jnp.concatenate([halo[0, y0], halo[0, y1]], 1),
+                    jnp.concatenate([halo[1, y0], halo[1, y1]], 1),
+                ],
+                0,
+            )
+            eh, el = split(edge)
+            ox = dot(core_x[...], jnp.concatenate([high, low, high, eh, el, eh, el], 0))
             oz = dot(
                 jnp.concatenate(
                     [
@@ -216,39 +227,11 @@
                 ),
                 core_z[...],
             )
-            before = field[lax.rem(y0 + cy - 1, cy)]
-            after = field[lax.rem(y1 + 1, cy)]
-            ox = ox[:cx] + ox[cx:]
+            before = field[(y0 + cy - 1) % cy]
+            after = field[(y1 + 1) % cy]
             oz = oz[:, :cz] + oz[:, cz:]
-            out[y0] = ox[:, :cz] + (before + b - 2.0 * a) + oz[:cx]
-            out[y1] = ox[:, cz:] + (a + after - 2.0 * b) + oz[cx:]
-            return carry
-
-        lax.fori_loop(0, cy // 2, body, 0, unroll=2)
-
-    def with_rim(halo, lap, use, out, keep):
-        def body(i, carry):
-            y0 = 2 * i
-            y1 = y0 + 1
-            edge = jnp.concatenate(
-                [
-                    jnp.concatenate([halo[0, y0], halo[0, y1]], 1),
-                    jnp.concatenate([halo[1, y0], halo[1, y1]], 1),
-                ],
-                0,
-            )
-            ox = dot(rim_x[...], jnp.concatenate(split(edge), 0))
-            ox = ox[:cx] + ox[cx:]
-            laps = (lap[y0] + ox[:, :cz], lap[y1] + ox[:, cz:])
-            nexts = [use(y, value) for y, value in zip((y0, y1), laps)]
-            for y, value, new in zip((y0, y1), laps, nexts):
-                if keep is not None:
-                    keep[y] = value
-                if new is not None:
-                    out[y] = new
-            return carry
-
-        lax.fori_loop(0, cy // 2, body, 0, unroll=2)
+            use(y0, a, ox[:, :cz] + oz[:cx] + (before + b))
+            use(y1, b, ox[:, cz:] + oz[cx:] + (a + after))
 
     def expand(coefs, out):
         for a in range(pairs):
@@ -282,8 +265,8 @@
         return carry
 
     lax.fori_loop(0, cy, source, 0, unroll=2)
-    to_planes(2, pf.at[0])
-    to_planes(3, qf.at[0])
+    to_steps(2, pf.at[1], dp)
+    to_steps(3, qf.at[1], dq)
     for copy in matrix_loads:
         copy.wait()
     finish(coef_rims)
@@ -296,31 +279,28 @@
 
     lax.fori_loop(0, cy, square, 0)
 
-    def step(t, carry):
-        core(pf.at[t + 1], lp.at[t])
-        core(qf.at[t + 1], lq)
+    for t in range(steps):
         finish(p_halo(t))
         scale = wave[t]
 
-        def use_p(y, lap):
-            return 2.0 * pf[t + 1, y] - pf[t, y] + sig2[y] * lap + scale * src[y]
-
-        with_rim(ph.at[t], lp.at[t], use_p, pf.at[t + 2], lp.at[t])
+        def use_p(y, now, lap):
+            lp[t, y] = lap
+            moved = dp[y] + sig2[y] * lap + scale * src[y]
+            dp[y] = moved
+            pf[t + 2, y] = now + moved
+
+        laplace(pf.at[t + 1], ph.at[t], use_p)
         start(p_halo(t + 1))
         finish(q_halo(t))
 
-        def use_q(y, lap):
-            return 2.0 * qf[t + 1, y] - qf[t, y] + sig2[y] * lap
-
-        with_rim(qh.at[t], lq, use_q, qf.at[t + 2], None)
-
-        @pl.when(t < steps - 1)
-        def _():
+        def use_q(y, now, lap):
+            moved = dq[y] + sig2[y] * lap
+            dq[y] = moved
+            qf[t + 2, y] = now + moved
+
+        laplace(qf.at[t + 1], qh.at[t], use_q)
+        if t < steps - 1:
             start(q_halo(t + 1))
-
-        return carry
-
-    lax.fori_loop(0, steps, step, 0)
 
     def image(i, carry):
         at = pl.ds(pl.multiple_of(i * 8, 8), 8)
@@ -346,7 +326,6 @@
         part0.at[:, cxc:, :], rims.at[0], part0.at[:, : 2 * OV, :], rims.at[1], ri_s, ri_r
     )
     start(part_rims)
-    core(pf.at[steps + 1], lp.at[steps])
     finish(part_rims)
     halfs = ext // rows
     for a in range(pairs):
@@ -375,7 +354,10 @@
         scatter.append(copy)
     finish(p_halo(steps))
 
-    with_rim(ph.at[steps], lp.at[steps], lambda y, lap: None, None, lp.at[steps])
+    def keep_lap(y, now, lap):
+        lp[steps, y] = lap
+
+    laplace(pf.at[steps + 1], ph.at[steps], keep_lap)
     mine = part[shot]
     for d in range(1, n_shot):
         scatter[d - 1].wait()
@@ -440,7 +422,7 @@
     for y in range(cy):
         speed = sig[y] - moved * exp_t[y]
         p_last[pl.ds(y, cx, stride=cy), :] = (
-            2.0 * pf[steps + 1, y] - pf[steps, y] + speed * speed * lp[steps, y] + last * src[y]
+            pf[steps + 1, y] + dp[y] + speed * speed * lp[steps, y] + last * src[y]
         )
 
 
@@ -476,7 +458,7 @@
         out_specs=(vmem, vmem),
         scratch_shapes=[
             buf(4, cx * cy, cz), sem(4),
-            buf(steps + 2, *field), buf(steps + 2, *field), buf(steps + 1, *field), buf(*field),
+            buf(steps + 2, *field), buf(steps + 2, *field), buf(steps + 1, *field), buf(*field), buf(*field),
             buf(*field), buf(*field), buf(*field), buf(cyc, cx, cz), buf(*field),
             buf(steps + 1, 2, cy, OV, cz), buf(steps, 2, cy, OV, cz),
             buf(pairs, ext, 128), buf(cyc, cx, cz), buf(pairs, ext, 128),

time: 48.8 us -> 43.2 us (0.89)
  Pallas kernels: 45.7 us -> 40.1 us
    pallas_call x1, Pallas kernels: 45.7 us -> 40.1 us  [on_device(): pl.pallas_call(functools.partial(kernel, dims, n_shot, n_tile, spline_y),...]
where the time goes in v1:
time: 43.2 us; the launch traced here: 43 us
  Pallas kernels  40.1 us (93%)
  local copies, waits for them, and re-layouts  2.29 us (5%)
  between operations  0.67 us (2%)
    pallas_call x1, Pallas kernels, on_device(): pl.pallas_call(functools.partial(kernel, dims, n_shot, n_tile, spline_y),...  40.1 us
    unnamed x8, local copies, waits for them, and re-layouts  2.29 us

profile of v1, /device:TPU:0, one launch (start us, length us, event | category | flops | bytes accessed | tf_op | source)
XLA Modules:
  0.0 43.0 jit_solution(14250784885829799187)
XLA Ops:
  0.6 0.0 copy-start
  0.6 0.0 copy-start.1
  0.7 0.0 copy-start.2
  0.7 0.6 %copy-done = s32[1,64]{1,0:T(1,128)S(1)} copy-done((s32[1,64]{1,0:T(1,128)S(1)}, s32[1,64]{1,0:T(1,128)}, u32[]{:S(2)}) %copy-start) | copy-done | bytes 280
  1.3 0.0 copy-done.1
  1.3 0.0 copy-done.2
  1.3 40.1 %shard_map.149 = (f32[64,512]{1,0:T(8,128)S(1)}, f32[2048,128]{1,0:T(8,128)S(1)}) custom-call(f32[2048,128]{1,0:T(8,128)} %bitcast.8, f32[2048,128]{1,0:T(8,128)} %bitcast.9, f32[2048,128]{1,0:T(8,128)} %bitcast.10, f32[2048,128]{1,0:T(8,128)} %bitcast.11, f32[64,512]{1,0:T(8,128)} %coef_in.1, s32[1,64]{1,0:T(1,128)S(1)} %copy-done, s32[1,64]{1,0:T(1,128)S(1)} %bitcast.7, ...), custom_call_target="tpu_custom_call" | custom-call | tf_op jit(solution)/shard_map/pallas_call | solution.py:448
  41.4 0.7 %copy.18 = f32[64,512]{1,0:T(8,128)} copy(f32[64,512]{1,0:T(8,128)S(1)} %get-tuple-element.8) | data formatting | bytes 262144
  42.1 1.0 %copy.19 = f32[1,128,16,128]{3,2,1,0:T(8,128)} copy(f32[1,128,16,128]{3,2,1,0:T(8,128)S(1)} %bitcast.6) | data formatting | bytes 2097152
Async XLA Ops:
  0.6 0.7 %copy-start = (s32[1,64]{1,0:T(1,128)S(1)}, s32[1,64]{1,0:T(1,128)}, u32[]{:S(2)}) copy-start(s32[1,64]{1,0:T(1,128)} %signs.1) | copy-start | bytes 772
  0.6 0.7 %copy-start.1 = (s32[64]{0:T(128)S(1)}, s32[64]{0:T(128)}, u32[]{:S(2)}) copy-start(s32[64]{0:T(128)} %param.20) | copy-start | bytes 772
  0.7 0.7 %copy-start.2 = (f32[5]{0:T(128)S(1)}, f32[5]{0:T(128)}, u32[]{:S(2)}) copy-start(f32[5]{0:T(128)} %wave.1) | copy-start | bytes 64

commit v2 on v1

v2 whole, which is shorter than its diff:
```python
import functools

import jax
import jax.numpy as jnp
import ml_dtypes
import numpy as np
from jax import lax
from jax.experimental import pallas as pl
from jax.experimental.pallas import tpu as pltpu
from jax.sharding import PartitionSpec as P

OV = 8
CHUNKS = 2
LEARN = 0.02
EPSILON = 1e-06
F32 = jnp.float32
BF16 = jnp.bfloat16
MESH = pl.DeviceIdType.MESH


def spectral_second(length):
    index = np.arange(length)
    number = np.minimum(index, length - index) * (2.0 * np.pi / length)
    gap = (index[:, None] - index[None, :])[:, :, None] * index[None, None, :] % length
    return np.sum(-(number * number) / length * np.cos(2.0 * np.pi / length * gap), axis=-1)


def spline_weight(offset):
    mag = np.abs(offset)
    inner = 2.0 / 3.0 - mag * mag + 0.5 * mag * mag * mag
    outer = (2.0 - mag) ** 3 / 6.0
    return np.where(mag < 1.0, inner, np.where(mag < 2.0, outer, 0.0))


def periodic_spline(fine, coarse):
    gap = np.arange(fine)[:, None] - 2 * np.arange(coarse)[None, :]
    return sum(spline_weight((gap + image * fine - 0.5) * 0.5) for image in range(-2, 3))


def halves(matrix):
    high = matrix.astype(np.float32).astype(ml_dtypes.bfloat16)
    low = (matrix - high.astype(np.float64)).astype(ml_dtypes.bfloat16)
    return high, low


def twice(block):
    out = np.zeros((2 * block.shape[0], 2 * block.shape[1]))
    out[: block.shape[0], : block.shape[1]] = block
    out[block.shape[0] :, block.shape[1] :] = block
    return out


def constants(cx, cz, cxc, czc):
    full = cx + 2 * OV
    ramp = np.sin(0.5 * np.pi * (np.arange(OV) + 0.5) / OV) ** 2
    second_x = spectral_second(full)[OV : OV + cx]
    high, low = halves(second_x[:, OV : OV + cx] - 2.0 * np.eye(cx))
    rim = np.concatenate([second_x[:, :OV] * ramp, second_x[:, OV + cx :] * ramp[::-1]], 1)
    rim_high, rim_low = halves(rim)
    core_x = np.concatenate([high, high, low, rim_high, rim_high, rim_low, rim_low], 1)
    high, low = halves(spectral_second(cz))
    core_z = np.block([[high, low], [high, low]])
    gap = np.arange(cx)[:, None] - 2 * (np.arange(cxc + 2 * OV)[None, :] - OV)
    expand_x = spline_weight((gap - 0.5) * 0.5)
    spline_z = periodic_spline(cz, czc)
    across = lambda m: np.concatenate([*(halves(m)[:1] * 2), halves(m)[1]], 1)
    down = lambda m: np.concatenate([*(halves(m)[:1] * 2), halves(m)[1]], 0)
    return [core_x, core_z, across(expand_x), down(twice(spline_z.T)), across(expand_x.T), down(twice(spline_z))]


def split(value):
    high = value.astype(BF16)
    return high, (value - high.astype(F32)).astype(BF16)


def dot(a, b):
    return jnp.dot(a, b, preferred_element_type=F32)


def kernel(
    dims, n_shot, n_tile, spline_y,
    p_now, p_prev, q_now, q_next, coef_in, signs_in, elems_in, wave_in,
    core_x_in, core_z_in, exp_x_in, exp_z_in, pro_x_in, pro_z_in,
    base, lap_last, sig, exp_t, ttot, scale_out,
    raw_sem, pf, qf, pv, qv, lp, dp, dq, acc, sig2, src, wide,
    ph, qh, cext, narrow, part0, rims, rs, tot, sq_all,
    ph_s, ph_r, qh_s, qh_r, ce_s, ce_r, ri_s, ri_r, rs_s, rs_r, ag_s, ag_r, sq_s, sq_r,
    tile_sem, shot_sem, consts_sem, signs, elems, wave, coef,
    core_x, core_z, exp_x, exp_z, pro_x, pro_z,
):
    cx, cy, cz, cxc, pairs, steps, group, rows, chunks = dims
    width = cy // chunks
    shot = lax.axis_index("shot")
    tile = lax.axis_index("tile")
    has_left = tile > 0
    has_right = tile < n_tile - 1
    ext = cxc + 2 * OV

    def across(bit):
        return shot + bit - 2 * bit * lax.rem(lax.div(shot, bit), 2)

    barrier = pltpu.get_barrier_semaphore()
    bits = [1 << b for b in range((n_shot - 1).bit_length())]
    reaches = [1 << b for b in range((n_tile - 2).bit_length())]

    def greet(right, left, reach):
        @pl.when(tile < n_tile - reach)
        def _():
            pl.semaphore_signal(
                right, inc=1, device_id={"tile": lax.rem(tile + reach, n_tile)}, device_id_type=MESH
            )

        @pl.when(tile >= reach)
        def _():
            pl.semaphore_signal(
                left, inc=1, device_id={"tile": lax.rem(tile + n_tile - reach, n_tile)}, device_id_type=MESH
            )

    greet(barrier, barrier, 1)
    for bit in bits:
        pl.semaphore_signal(barrier, inc=1, device_id={"shot": across(bit)}, device_id_type=MESH)

    def tell(i):
        if i < len(reaches):
            greet(tile_sem.at[i, 0], tile_sem.at[i, 1], reaches[i])
        elif i < len(reaches) + len(bits):
            at = i - len(reaches)
            pl.semaphore_signal(shot_sem.at[at], inc=1, device_id={"shot": across(bits[at])}, device_id_type=MESH)

    def hear(i):
        if i < len(reaches):
            @pl.when(tile >= reaches[i])
            def _():
                pl.semaphore_wait(tile_sem.at[i, 0], 1)

            @pl.when(tile < n_tile - reaches[i])
            def _():
                pl.semaphore_wait(tile_sem.at[i, 1], 1)
        elif i < len(reaches) + len(bits):
            pl.semaphore_wait(shot_sem.at[i - len(reaches)], 1)

    def load(ref, out, s):
        copy = pltpu.make_async_copy(ref, out, s)
        copy.start()
        return copy

    fields = ((p_now, pf.at[1]), (q_now, qf.at[1]), (p_prev, pv), (q_next, qv))
    matrices = (
        (coef_in, coef), (signs_in, signs), (elems_in, elems), (wave_in, wave),
        (core_x_in, core_x), (core_z_in, core_z), (exp_x_in, exp_x),
        (exp_z_in, exp_z), (pro_x_in, pro_x), (pro_z_in, pro_z),
    )

    def load_planes(i):
        for y in range(cy):
            pltpu.make_async_copy(fields[i][0].at[:, y, :], fields[i][1].at[y], raw_sem.at[i]).start()

    def loaded(i):
        pltpu.make_async_copy(fields[i][1], fields[i][1], raw_sem.at[i]).wait()

    load_planes(0)
    load_planes(1)
    small = [load(a, b, consts_sem.at[i]) for i, (a, b) in enumerate(matrices)]
    load_planes(2)
    load_planes(3)

    @pl.when(jnp.logical_not(has_left))
    def _():
        ph[:, 0] = jnp.zeros_like(ph[:, 0])
        qh[:, 0] = jnp.zeros_like(qh[:, 0])
        cext[:, :OV, :] = jnp.zeros((pairs, OV, 128), F32)
        rims[0] = jnp.zeros_like(rims[0])

    @pl.when(jnp.logical_not(has_right))
    def _():
        ph[:, 1] = jnp.zeros_like(ph[:, 1])
        qh[:, 1] = jnp.zeros_like(qh[:, 1])
        cext[:, OV + cxc :, :] = jnp.zeros((pairs, OV, 128), F32)
        rims[1] = jnp.zeros_like(rims[1])

    def beside(to_right, right_dst, to_left, left_dst, ss, rr):
        right = pltpu.make_async_remote_copy(
            src_ref=to_right, dst_ref=right_dst, send_sem=ss.at[0], recv_sem=rr.at[0],
            device_id={"tile": lax.rem(tile + 1, n_tile)}, device_id_type=MESH,
        )
        left = pltpu.make_async_remote_copy(
            src_ref=to_left, dst_ref=left_dst, send_sem=ss.at[1], recv_sem=rr.at[1],
            device_id={"tile": lax.rem(tile + n_tile - 1, n_tile)}, device_id_type=MESH,
        )
        return right, left

    def start(pair):
        @pl.when(has_right)
        def _():
            pair[0].start()

        @pl.when(has_left)
        def _():
            pair[1].start()

    def finish(pair):
        @pl.when(has_right)
        def _():
            pair[0].wait_send()
            pair[1].wait_recv()

        @pl.when(has_left)
        def _():
            pair[1].wait_send()
            pair[0].wait_recv()

    def field_halo(field, index, halo, t, c, ss, rr):
        planes = pl.ds(c * width, width)
        return beside(
            field.at[index, planes, cx - OV :, :], halo.at[t, 0, planes],
            field.at[index, planes, :OV, :], halo.at[t, 1, planes], ss.at[t, c], rr.at[t, c],
        )

    p_halo = lambda t, c: field_halo(pf, t + 1, ph, t, c, ph_s, ph_r)
    q_halo = lambda t, c: field_halo(qf, t + 1, qh, t, c, qh_s, qh_r)

    def arrive(pair):
        @pl.when(has_right)
        def _():
            pair[1].wait_recv()

        @pl.when(has_left)
        def _():
            pair[0].wait_recv()

    def sent(pairs):
        @pl.when(has_right)
        def _():
            for pair in pairs:
                pair[0].wait_send()

        @pl.when(has_left)
        def _():
            for pair in pairs:
                pair[1].wait_send()

    beside_count = 1 - lax.div(tile + 1, n_tile) + lax.div(tile + n_tile - 1, n_tile)
    pl.semaphore_wait(barrier, len(bits) + beside_count)
    loaded(0)
    for c in range(chunks):
        start(p_halo(0, c))
    loaded(1)
    for c in range(chunks):
        start(q_halo(0, c))
    tell(0)
    for copy in small[:4]:
        copy.wait()
    for a in range(pairs):
        cext[a, OV : OV + cxc, :] = coef[:, a * 128 : (a + 1) * 128]
    coef_rims = beside(
        cext.at[:, cxc : cxc + OV, :], cext.at[:, :OV, :],
        cext.at[:, OV : 2 * OV, :], cext.at[:, OV + cxc :, :], ce_s, ce_r,
    )
    start(coef_rims)

    def laplace(field, halo, c, use):
        for i in range(c * width // 2, (c + 1) * width // 2):
            y0, y1 = 2 * i, 2 * i + 1
            a = field[y0]
            b = field[y1]
            high, low = split(jnp.concatenate([a, b], 1))
            edge = jnp.concatenate(
                [
                    jnp.concatenate([halo[0, y0], halo[0, y1]], 1),
                    jnp.concatenate([halo[1, y0], halo[1, y1]], 1),
                ],
                0,
            )
            eh, el = split(edge)
            ox = dot(core_x[...], jnp.concatenate([high, low, high, eh, el, eh, el], 0))
            oz = dot(
                jnp.concatenate(
                    [
                        jnp.concatenate([high[:, :cz], low[:, :cz]], 1),
                        jnp.concatenate([high[:, cz:], low[:, cz:]], 1),
                    ],
                    0,
                ),
                core_z[...],
            )
            before = field[(y0 + cy - 1) % cy]
            after = field[(y1 + 1) % cy]
            oz = oz[:, :cz] + oz[:, cz:]
            use(y0, a, ox[:, :cz] + oz[:cx] + (before + b))
            use(y1, b, ox[:, cz:] + oz[cx:] + (a + after))

    def expand(coefs, out):
        tall = []
        for a in range(0, pairs, 2):
            high, low = split(jnp.concatenate([coefs[a], coefs[a + 1]], 1))
            both = dot(exp_x[...], jnp.concatenate([high, low, high], 0))
            tall += [both[:, :128], both[:, 128:]]
        high, low = split(jnp.concatenate(tall, 0))
        both = dot(jnp.concatenate([high, low, high], 1), exp_z[...])
        for a in range(pairs):
            wide[2 * a] = both[a * cx : (a + 1) * cx, :cz]
            wide[2 * a + 1] = both[a * cx : (a + 1) * cx, cz:]

        def body(i, carry):
            at = pl.ds(pl.multiple_of(i * 8, 8), 8)
            planes = [wide[j, at, :] for j in range(2 * pairs)]
            for y in range(cy):
                terms = [
                    float(spline_y[y, j]) * planes[j] for j in range(2 * pairs) if spline_y[y, j] != 0
                ]
                out[y, at, :] = functools.reduce(lambda u, v: u + v, terms)
            return carry

        lax.fori_loop(0, cx // 8, body, 0)

    count = elems.shape[1]
    where_to = elems[...]
    amount = (2 * signs[...] - 1).astype(F32)
    row_of = lax.rem(lax.div(where_to, cz), cy) * cx + lax.div(where_to, cz * cy)
    lanes = (lax.broadcasted_iota(jnp.int32, (cz, count), 0) == lax.rem(where_to, cz)).astype(F32)
    lanes = lanes.astype(BF16)

    def source(y, carry):
        place = lax.broadcasted_iota(jnp.int32, (cx, count), 0) + y * cx
        hits = jnp.where(place == row_of, amount, 0.0).astype(BF16)
        src[y] = lax.dot_general(hits, lanes, (((1,), (1,)), ((), ())), preferred_element_type=F32)
        return carry

    lax.fori_loop(0, cy, source, 0, unroll=2)
    for copy in small[4:]:
        copy.wait()
    finish(coef_rims)
    expand(cext, sig)

    def square(y, carry):
        value = sig[y]
        sig2[y] = value * value
        return carry

    lax.fori_loop(0, cy, square, 0)

    loaded(2)
    loaded(3)
    for t in range(steps):
        scale = wave[t]

        def use_p(y, now, lap):
            if t < steps - 1:
                lp[t, y] = lap
            else:
                total = qf[2, y] * lap
                for u in range(1, steps - 1):
                    total = total + qf[steps + 1 - u, y] * lp[u, y]
                acc[y] = total
            step = dp[y] if t > 0 else now - pv[y]
            moved = step + sig2[y] * lap + scale * src[y]
            dp[y] = moved
            pf[t + 2, y] = now + moved

        def use_q(y, now, lap):
            step = dq[y] if t > 0 else now - qv[y]
            moved = step + sig2[y] * lap
            if t < steps - 1:
                dq[y] = moved
            qf[t + 2, y] = now + moved

        for c in range(chunks):
            arrive(p_halo(t, c))
            laplace(pf.at[t + 1], ph.at[t], c, use_p)
            start(p_halo(t + 1, c))
        hear(2 * t)
        tell(2 * t + 1)
        for c in range(chunks):
            arrive(q_halo(t, c))
            laplace(qf.at[t + 1], qh.at[t], c, use_q)
            if t < steps - 1:
                start(q_halo(t + 1, c))
        hear(2 * t + 1)
        tell(2 * t + 2)
    for i in range(2 * steps, len(reaches) + len(bits)):
        hear(i)
        tell(i + 1)

    def image(i, carry):
        at = pl.ds(pl.multiple_of(i * 8, 8), 8)
        out = [None] * (2 * pairs)
        for y in range(cy):
            value = sig[y, at, :] * (acc[y, at, :] + qf[steps + 1, y, at, :] * lp[0, y, at, :])
            for j in range(2 * pairs):
                if spline_y[y, j] != 0:
                    term = float(2.0 * spline_y[y, j]) * value
                    out[j] = term if out[j] is None else out[j] + term
        for j in range(2 * pairs):
            narrow[j, at, :] = out[j]
        return carry

    lax.fori_loop(0, cx // 8, image, 0, unroll=2)
    tall = []
    for a in range(pairs):
        high, low = split(jnp.concatenate([narrow[2 * a], narrow[2 * a + 1]], 1))
        tall.append(dot(pro_x[...], jnp.concatenate([high, low, high], 0)))
    high, low = split(jnp.concatenate(tall, 0))
    tall = dot(jnp.concatenate([high, low, high], 1), pro_z[...])
    for a in range(pairs):
        part0[a] = tall[a * ext : (a + 1) * ext]
    halfs = ext // rows

    def piece(s):
        return pl.ds(s * group // halfs, group), pl.ds(lax.rem(s, halfs) * rows, rows)

    rim_sends = []
    for d in range(n_shot):
        to = lax.rem(shot + d, n_shot)
        own = pl.ds(to * group // halfs, group)
        pair = []
        for side, (first, step) in enumerate(((cxc, 1), (0, n_tile - 1))):
            pair.append(pltpu.make_async_remote_copy(
                src_ref=part0.at[own, pl.ds(first, 2 * OV), :], dst_ref=rims.at[side, d],
                send_sem=ri_s.at[side, d], recv_sem=ri_r.at[side, d],
                device_id={"shot": to, "tile": lax.rem(tile + step, n_tile)}, device_id_type=MESH,
            ))
        rim_sends.append(pair)

    def peer_copy(source_ref, target_ref, d, ss, rr):
        return pltpu.make_async_remote_copy(
            src_ref=source_ref, dst_ref=target_ref, send_sem=ss.at[d - 1], recv_sem=rr.at[d - 1],
            device_id={"shot": lax.rem(shot + d, n_shot)}, device_id_type=MESH,
        )

    scatter = []
    for d in range(1, n_shot):
        planes, lines = piece(lax.rem(shot + d, n_shot))
        copy = peer_copy(part0.at[planes, lines, :], rs.at[d - 1], d, rs_s, rs_r)
        copy.start()
        scatter.append(copy)

    @pl.when(has_right)
    def _():
        for pair in rim_sends:
            pair[0].start()

    @pl.when(has_left)
    def _():
        for pair in rim_sends:
            pair[1].start()

    def keep_lap(y, now, lap):
        lap_last[y] = lap

    def last_lap(c):
        arrive(p_halo(steps, c))
        laplace(pf.at[steps + 1], ph.at[steps], c, keep_lap)

    for c in range(chunks // 2):
        last_lap(c)
    planes, lines = piece(shot)
    mine = part0[planes, lines, :]
    for d in range(1, n_shot):
        scatter[d - 1].wait()
        mine = mine + rs[d - 1]

    @pl.when(has_right)
    def _():
        for pair in rim_sends:
            pair[0].wait_send()
            pair[1].wait_recv()

    @pl.when(has_left)
    def _():
        for pair in rim_sends:
            pair[1].wait_send()
            pair[0].wait_recv()

    place = lax.rem(shot, halfs)
    low_rim = functools.reduce(lambda u, v: u + v, [rims[0, d] for d in range(n_shot)])
    high_rim = functools.reduce(lambda u, v: u + v, [rims[1, d] for d in range(n_shot)])
    low_rim = low_rim * jnp.where(place == 0, 1.0, 0.0).astype(F32)
    high_rim = high_rim * jnp.where(place == halfs - 1, 1.0, 0.0).astype(F32)
    none = jnp.zeros((group, rows - 2 * OV, 128), F32)
    mine = mine + jnp.concatenate([low_rim, none], 1) + jnp.concatenate([none, high_rim], 1)
    tot[shot] = mine
    gather = []
    for d in range(1, n_shot):
        copy = peer_copy(tot.at[shot], tot.at[shot], d, ag_s, ag_r)
        copy.start()
        gather.append(copy)
    squares = jnp.zeros((8, 128), F32)
    first = lax.rem(shot, halfs) * rows
    for g in range(group):
        for r in range(0, rows, 8):
            inside = jnp.logical_and(first + r >= OV, first + r < OV + cxc)
            value = mine[g, r : r + 8] * jnp.where(inside, 1.0, 0.0).astype(F32)
            squares = squares + value * mine[g, r : r + 8]
    sq_all[0] = jnp.sum(squares, axis=0, keepdims=True)
    for d in range(n_shot * n_tile - 1, 0, -1):
        pltpu.make_async_remote_copy(
            src_ref=sq_all.at[0], dst_ref=sq_all.at[d], send_sem=sq_s, recv_sem=sq_r,
            device_id={
                "shot": lax.rem(shot + d // n_tile, n_shot), "tile": lax.rem(tile + d % n_tile, n_tile)
            },
            device_id_type=MESH,
        ).start()
    last = wave[steps]
    for y in range(cy):
        base[y] = pf[steps + 1, y] + dp[y] + last * src[y]
    for c in range(chunks // 2, chunks):
        last_lap(c)
    for copy in gather:
        copy.wait()
    left_on = jnp.where(has_left, 1.0, 0.0).astype(F32)
    right_on = jnp.where(has_right, 1.0, 0.0).astype(F32)
    for a in range(pairs):
        pieces = []
        for r in range(halfs):
            flat = a * halfs + r
            pieces.append(tot[flat // group, flat % group])
        whole = pieces[0] if halfs == 1 else jnp.concatenate(pieces, 0)
        ttot[a, :OV, :] = whole[:OV] * left_on
        ttot[a, OV : OV + cxc, :] = whole[OV : OV + cxc]
        ttot[a, OV + cxc :, :] = whole[OV + cxc :] * right_on
    expand(ttot, exp_t)
    sent([p_halo(t, c) for t in range(steps + 1) for c in range(chunks)])
    sent([q_halo(t, c) for t in range(steps) for c in range(chunks)])
    others = sq_all.at[pl.ds(1, n_shot * n_tile - 1)]
    everyone = pltpu.make_async_remote_copy(
        src_ref=others, dst_ref=others, send_sem=sq_s, recv_sem=sq_r,
        device_id={"shot": across(1)}, device_id_type=MESH,
    )
    everyone.wait_send()
    everyone.wait_recv()
    cells = float(n_tile * cxc * 2 * pairs * 64)
    mean = jnp.sum(jnp.sum(sq_all[...], axis=0), axis=1, keepdims=True) / cells
    scale_out[...] = jnp.broadcast_to(1.0 / jnp.sqrt(mean + EPSILON), scale_out.shape)


def finish_kernel(base, lap_last, sig, exp_t, ttot, scale_in, direction, p_last, turned, done, dir_sem, out_sem):
    pairs = ttot.shape[0]
    cxc = direction.shape[0]
    scale = scale_in[...]
    for a in range(pairs):
        turned[:, a * 128 : (a + 1) * 128] = ttot[a, OV : OV + cxc, :] * scale
    copies = [pltpu.make_async_copy(turned, direction, dir_sem)]
    copies[0].start()
    moved = LEARN * scale
    for y in range(base.shape[0]):
        speed = sig[y] - moved * exp_t[y]
        done[y] = base[y] + speed * speed * lap_last[y]
        copies.append(pltpu.make_async_copy(done.at[y], p_last.at[:, y, :], out_sem.at[y]))
        copies[-1].start()
    for copy in copies:
        copy.wait()


def on_device(n_shot, n_tile, p_now, p_prev, adj_now, adj_next, coef_old, signs, elem_index, wavelet):
    _, cx, cy, cz = p_now.shape
    cxc, merged = coef_old.shape
    steps = wavelet.shape[0] - 1
    cyc = cy // 2
    czc = merged // cyc
    pairs = cyc // 2
    spline_y = periodic_spline(cy, cyc).astype(np.float32)
    ext = cxc + 2 * OV
    group = max(1, pairs // n_shot)
    rows = ext // max(1, n_shot // pairs)
    dims = (cx, cy, cz, cxc, pairs, steps, group, rows, CHUNKS)
    consts = [jnp.asarray(c) for c in constants(cx, cz, cxc, czc)]
    vmem = pl.BlockSpec(memory_space=pltpu.VMEM)
    hbm = pl.BlockSpec(memory_space=pltpu.HBM)
    held = lambda v: pltpu.with_memory_space_constraint(v, pltpu.HBM)
    field = (cy, cx, cz)
    buf = lambda *shape: pltpu.VMEM(shape, F32)
    sem = lambda *shape: pltpu.SemaphoreType.DMA(shape)
    like = lambda *shape: jax.ShapeDtypeStruct(shape, F32)
    state = pl.pallas_call(
        functools.partial(kernel, dims, n_shot, n_tile, spline_y),
        out_shape=(*[like(*field)] * 4, like(pairs, ext, 128), like(1, 128)),
        in_specs=[hbm] * (8 + len(consts)),
        out_specs=(vmem,) * 6,
        scratch_shapes=[
            sem(4), buf(steps + 2, *field), buf(steps + 2, *field), *[buf(*field)] * 2,
            buf(steps, *field), *[buf(*field)] * 5, buf(cyc, cx, cz),
            buf(steps + 1, 2, cy, OV, cz), buf(steps, 2, cy, OV, cz),
            buf(pairs, ext, 128), buf(cyc, cx, cz), buf(pairs, ext, 128),
            buf(2, n_shot, group, 2 * OV, 128), buf(max(1, n_shot - 1), group, rows, 128),
            buf(n_shot, group, rows, 128), buf(n_shot * n_tile, 1, 128),
            *[sem(steps + 1, CHUNKS, 2)] * 2, *[sem(steps, CHUNKS, 2)] * 2,
            sem(2), sem(2), sem(2, n_shot), sem(2, n_shot),
            *[sem(max(1, n_shot - 1))] * 4, sem(), sem(),
            pltpu.SemaphoreType.REGULAR((max(1, (n_tile - 2).bit_length()), 2)),
            pltpu.SemaphoreType.REGULAR((max(1, (n_shot - 1).bit_length()),)),
            sem(4 + len(consts)), pltpu.VMEM(signs.shape, jnp.int32), pltpu.VMEM(signs.shape, jnp.int32),
            pltpu.SMEM(wavelet.shape, F32), buf(cxc, merged),
        ]
        + [pltpu.VMEM(c.shape, c.dtype) for c in consts],
        compiler_params=pltpu.CompilerParams(
            collective_id=0, has_side_effects=True, vmem_limit_bytes=40 * 1024 * 1024
        ),
    )(
        *map(held, (p_now[0], p_prev[0], adj_now[0], adj_next[0], coef_old)),
        *map(held, (signs, elem_index.reshape(1, -1), wavelet)), *map(held, consts),
    )
    direction, p_last = pl.pallas_call(
        finish_kernel,
        out_shape=(like(cxc, merged), like(cx, cy, cz)),
        in_specs=[vmem] * 6,
        out_specs=(hbm, hbm),
        scratch_shapes=[buf(cxc, merged), buf(*field), sem(), sem(cy)],
        compiler_params=pltpu.CompilerParams(vmem_limit_bytes=12 * 1024 * 1024),
    )(*state)
    return direction, p_last[None]


def solution(mesh):
    placed = (
        P("shot", "tile", None, None),
        P("shot", "tile", None, None),
        P("shot", "tile", None, None),
        P("shot", "tile", None, None),
        P("tile", None),
        P("shot", "tile"),
        P("tile"),
        P(),
    )
    return jax.shard_map(
        functools.partial(on_device, mesh.shape["shot"], mesh.shape["tile"]),
        mesh=mesh,
        in_specs=placed,
        out_specs=(P("tile", None), P("shot", "tile", None, None)),
        check_vma=False,
    )
```

time: 43.2 us -> 34 us (0.79)
  Pallas kernels: 40.1 us -> 33.2 us
  local copies, waits for them, and re-layouts: 2.29 us -> 0 us
    pallas_call x1, Pallas kernels: 40.1 us -> 32 us  [on_device(): pl.pallas_call(functools.partial(kernel, dims, n_shot, n_tile, spline_y),...]
    unnamed x8 -> x0, local copies, waits for them, and re-layouts: 2.29 us -> none
    pallas_call x0 -> x1, Pallas kernels: none -> 1.17 us  [on_device(): pl.pallas_call(finish_kernel, out_shape=(like(cxc, merged), like(cx, cy,...]
where the time goes in v2:
time: 34 us; the launch traced here: 33.8 us
  Pallas kernels  33.2 us (98%)
  between operations  0.64 us (2%)
    pallas_call x1, Pallas kernels, on_device(): pl.pallas_call(functools.partial(kernel, dims, n_shot, n_tile, spline_y),...  32 us
    pallas_call x1, Pallas kernels, on_device(): pl.pallas_call(finish_kernel, out_shape=(like(cxc, merged), like(cx, cy,...  1.17 us

profile of v2, /device:TPU:0, one launch (start us, length us, event | category | flops | bytes accessed | tf_op | source)
XLA Modules:
  0.0 33.8 jit_solution(244403779411055437)
XLA Ops:
  0.6 32.0 %shard_map.149 = (f32[16,128,128]{2,1,0:T(8,128)S(1)}, f32[16,128,128]{2,1,0:T(8,128)S(1)}, f32[16,128,128]{2,1,0:T(8,128)S(1)}, f32[16,128,128]{2,1,0:T(8,128)S...) custom-call(f32[128,16,128]{2,1,0:T(8,128)} %bitcast.6, f32[128,16,128]{2,1,0:T(8,128)} %bitcast.7, ...), custom_call_target="tpu_custom_call" | custom-call | tf_op jit(solution)/shard_map/pallas_call | solution.py:574
  32.7 1.2 %shard_map.150 = (f32[64,512]{1,0:T(8,128)}, f32[128,16,128]{2,1,0:T(8,128)}) custom-call(f32[16,128,128]{2,1,0:T(8,128)S(1)} %get-tuple-element.10.base, f32[16,128,128]{2,1,0:T(8,128)S(1)} %get-tuple-element.11.lap_last, f32[16,128,128]{2,1,0:T(8,128)S(1)} %get-tuple-element.12.sig, f32[16,128,128]{2,1,0:T(8,128)S(1)} %get-tuple-element.13.exp_t, ...), custom_call_target="tpu_custom_call" | custom-call | tf_op jit(solution)/shard_map/pallas_call | solution.py:602

commit v3 on v2

--- a/solution.py
+++ b/solution.py
@@ -10,7 +10,6 @@
 from jax.sharding import PartitionSpec as P
 
 OV = 8
-CHUNKS = 2
 LEARN = 0.02
 EPSILON = 1e-06
 F32 = jnp.float32
@@ -57,7 +56,9 @@
     high, low = halves(second_x[:, OV : OV + cx] - 2.0 * np.eye(cx))
     rim = np.concatenate([second_x[:, :OV] * ramp, second_x[:, OV + cx :] * ramp[::-1]], 1)
     rim_high, rim_low = halves(rim)
-    core_x = np.concatenate([high, high, low, rim_high, rim_high, rim_low, rim_low], 1)
+    core_x = np.concatenate([high, high, low], 1)
+    rim_x = np.concatenate([rim_high, rim_high, rim_low, rim_low], 1)
+    rim_edge = np.concatenate([rim_x[:OV], rim_x[cx - OV :]], 0)
     high, low = halves(spectral_second(cz))
     core_z = np.block([[high, low], [high, low]])
     gap = np.arange(cx)[:, None] - 2 * (np.arange(cxc + 2 * OV)[None, :] - OV)
@@ -65,7 +66,7 @@
     spline_z = periodic_spline(cz, czc)
     across = lambda m: np.concatenate([*(halves(m)[:1] * 2), halves(m)[1]], 1)
     down = lambda m: np.concatenate([*(halves(m)[:1] * 2), halves(m)[1]], 0)
-    return [core_x, core_z, across(expand_x), down(twice(spline_z.T)), across(expand_x.T), down(twice(spline_z))]
+    return [core_x, core_z, rim_x, rim_edge, across(expand_x), down(twice(spline_z.T)), across(expand_x.T), down(twice(spline_z))]
 
 
 def split(value):
@@ -80,16 +81,15 @@
 def kernel(
     dims, n_shot, n_tile, spline_y,
     p_now, p_prev, q_now, q_next, coef_in, signs_in, elems_in, wave_in,
-    core_x_in, core_z_in, exp_x_in, exp_z_in, pro_x_in, pro_z_in,
+    core_x_in, core_z_in, rim_x_in, rim_edge_in, exp_x_in, exp_z_in, pro_x_in, pro_z_in,
     base, lap_last, sig, exp_t, ttot, scale_out,
-    raw_sem, pf, qf, pv, qv, lp, dp, dq, acc, sig2, src, wide,
+    raw_sem, pf, qf, pv, qv, lp, dp, dq, acc, sig2, src, wide, cp, cq, ep, eq,
     ph, qh, cext, narrow, part0, rims, rs, tot, sq_all,
     ph_s, ph_r, qh_s, qh_r, ce_s, ce_r, ri_s, ri_r, rs_s, rs_r, ag_s, ag_r, sq_s, sq_r,
     tile_sem, shot_sem, consts_sem, signs, elems, wave, coef,
-    core_x, core_z, exp_x, exp_z, pro_x, pro_z,
+    core_x, core_z, rim_x, rim_edge, exp_x, exp_z, pro_x, pro_z,
 ):
-    cx, cy, cz, cxc, pairs, steps, group, rows, chunks = dims
-    width = cy // chunks
+    cx, cy, cz, cxc, pairs, steps, group, rows = dims
     shot = lax.axis_index("shot")
     tile = lax.axis_index("tile")
     has_left = tile > 0
@@ -147,7 +147,8 @@
     fields = ((p_now, pf.at[1]), (q_now, qf.at[1]), (p_prev, pv), (q_next, qv))
     matrices = (
         (coef_in, coef), (signs_in, signs), (elems_in, elems), (wave_in, wave),
-        (core_x_in, core_x), (core_z_in, core_z), (exp_x_in, exp_x),
+        (core_x_in, core_x), (core_z_in, core_z), (rim_x_in, rim_x), (rim_edge_in, rim_edge),
+        (exp_x_in, exp_x),
         (exp_z_in, exp_z), (pro_x_in, pro_x), (pro_z_in, pro_z),
     )
 
@@ -209,15 +210,13 @@
             pair[1].wait_send()
             pair[0].wait_recv()
 
-    def field_halo(field, index, halo, t, c, ss, rr):
-        planes = pl.ds(c * width, width)
-        return beside(
-            field.at[index, planes, cx - OV :, :], halo.at[t, 0, planes],
-            field.at[index, planes, :OV, :], halo.at[t, 1, planes], ss.at[t, c], rr.at[t, c],
-        )
-
-    p_halo = lambda t, c: field_halo(pf, t + 1, ph, t, c, ph_s, ph_r)
-    q_halo = lambda t, c: field_halo(qf, t + 1, qh, t, c, qh_s, qh_r)
+    def field_halo(field, edges, halo, t, ss, rr):
+        to_right = field.at[1, :, cx - OV :, :] if t == 0 else edges.at[t - 1, 0]
+        to_left = field.at[1, :, :OV, :] if t == 0 else edges.at[t - 1, 1]
+        return beside(to_right, halo.at[t, 0], to_left, halo.at[t, 1], ss.at[t], rr.at[t])
+
+    p_halo = lambda t: field_halo(pf, ep, ph, t, ph_s, ph_r)
+    q_halo = lambda t: field_halo(qf, eq, qh, t, qh_s, qh_r)
 
     def arrive(pair):
         @pl.when(has_right)
@@ -242,11 +241,9 @@
     beside_count = 1 - lax.div(tile + 1, n_tile) + lax.div(tile + n_tile - 1, n_tile)
     pl.semaphore_wait(barrier, len(bits) + beside_count)
     loaded(0)
-    for c in range(chunks):
-        start(p_halo(0, c))
+    start(p_halo(0))
     loaded(1)
-    for c in range(chunks):
-        start(q_halo(0, c))
+    start(q_halo(0))
     tell(0)
     for copy in small[:4]:
         copy.wait()
@@ -258,36 +255,61 @@
     )
     start(coef_rims)
 
-    def laplace(field, halo, c, use):
-        for i in range(c * width // 2, (c + 1) * width // 2):
-            y0, y1 = 2 * i, 2 * i + 1
-            a = field[y0]
-            b = field[y1]
-            high, low = split(jnp.concatenate([a, b], 1))
-            edge = jnp.concatenate(
+    def core(y0, a, b, out):
+        high, low = split(jnp.concatenate([a, b], 1))
+        ox = dot(core_x[...], jnp.concatenate([high, low, high], 0))
+        oz = dot(
+            jnp.concatenate(
                 [
-                    jnp.concatenate([halo[0, y0], halo[0, y1]], 1),
-                    jnp.concatenate([halo[1, y0], halo[1, y1]], 1),
+                    jnp.concatenate([high[:, :cz], low[:, :cz]], 1),
+                    jnp.concatenate([high[:, cz:], low[:, cz:]], 1),
                 ],
                 0,
-            )
-            eh, el = split(edge)
-            ox = dot(core_x[...], jnp.concatenate([high, low, high, eh, el, eh, el], 0))
-            oz = dot(
-                jnp.concatenate(
-                    [
-                        jnp.concatenate([high[:, :cz], low[:, :cz]], 1),
-                        jnp.concatenate([high[:, cz:], low[:, cz:]], 1),
-                    ],
-                    0,
-                ),
-                core_z[...],
-            )
-            before = field[(y0 + cy - 1) % cy]
-            after = field[(y1 + 1) % cy]
-            oz = oz[:, :cz] + oz[:, cz:]
-            use(y0, a, ox[:, :cz] + oz[:cx] + (before + b))
-            use(y1, b, ox[:, cz:] + oz[cx:] + (a + after))
+            ),
+            core_z[...],
+        )
+        oz = oz[:, :cz] + oz[:, cz:]
+        out[y0] = ox[:, :cz] + oz[:cx]
+        out[y0 + 1] = ox[:, cz:] + oz[cx:]
+
+    def cores(field, out):
+        for y in range(0, cy, 2):
+            core(y, field[y], field[y + 1], out)
+
+    def rim(matrix, halo, y):
+        edge = jnp.concatenate(
+            [
+                jnp.concatenate([halo[0, y], halo[0, y + 1]], 1),
+                jnp.concatenate([halo[1, y], halo[1, y + 1]], 1),
+            ],
+            0,
+        )
+        high, low = split(edge)
+        return dot(matrix[...], jnp.concatenate([high, low, high, low], 0))
+
+    def laplace(field, partial, halo, use, other=None, out=None):
+        for y in range(0, cy, 2):
+            a = field[y]
+            b = field[y + 1]
+            ox = rim(rim_x, halo, y)
+            before = field[(y + cy - 1) % cy]
+            after = field[(y + 2) % cy]
+            if other is not None:
+                core(y, other[y], other[y + 1], out)
+            use(y, a, partial[y] + ox[:, :cz] + (before + b))
+            use(y + 1, b, partial[y + 1] + ox[:, cz:] + (a + after))
+
+    def edges(field, partial, halo, use, out):
+        for y in range(0, cy, 2):
+            ox = rim(rim_edge, halo, y)
+            for side, at in ((1, slice(0, OV)), (0, slice(cx - OV, cx))):
+                a = field[y, at, :]
+                b = field[y + 1, at, :]
+                part = ox[:OV] if side else ox[OV:]
+                before = field[(y + cy - 1) % cy, at, :]
+                after = field[(y + 2) % cy, at, :]
+                out[side, y] = use(y, at, a, partial[y, at, :] + part[:, :cz] + (before + b))
+                out[side, y + 1] = use(y + 1, at, b, partial[y + 1, at, :] + part[:, cz:] + (a + after))
 
     def expand(coefs, out):
         tall = []
@@ -329,6 +351,7 @@
     lax.fori_loop(0, cy, source, 0, unroll=2)
     for copy in small[4:]:
         copy.wait()
+    cores(pf.at[1], cp)
     finish(coef_rims)
     expand(cext, sig)
 
@@ -343,6 +366,10 @@
     loaded(3)
     for t in range(steps):
         scale = wave[t]
+
+        def move_p(y, at, now, lap):
+            past = dp[y, at, :] if t > 0 else now - pv[y, at, :]
+            return past + sig2[y, at, :] * lap + scale * src[y, at, :]
 
         def use_p(y, now, lap):
             if t < steps - 1:
@@ -352,29 +379,31 @@
                 for u in range(1, steps - 1):
                     total = total + qf[steps + 1 - u, y] * lp[u, y]
                 acc[y] = total
-            step = dp[y] if t > 0 else now - pv[y]
-            moved = step + sig2[y] * lap + scale * src[y]
+            moved = move_p(y, slice(0, cx), now, lap)
             dp[y] = moved
             pf[t + 2, y] = now + moved
 
+        def move_q(y, at, now, lap):
+            past = dq[y, at, :] if t > 0 else now - qv[y, at, :]
+            return past + sig2[y, at, :] * lap
+
         def use_q(y, now, lap):
-            step = dq[y] if t > 0 else now - qv[y]
-            moved = step + sig2[y] * lap
+            moved = move_q(y, slice(0, cx), now, lap)
             if t < steps - 1:
                 dq[y] = moved
             qf[t + 2, y] = now + moved
 
-        for c in range(chunks):
-            arrive(p_halo(t, c))
-            laplace(pf.at[t + 1], ph.at[t], c, use_p)
-            start(p_halo(t + 1, c))
+        arrive(p_halo(t))
+        edges(pf.at[t + 1], cp, ph.at[t], lambda y, at, now, lap: now + move_p(y, at, now, lap), ep.at[t])
+        start(p_halo(t + 1))
+        laplace(pf.at[t + 1], cp, ph.at[t], use_p, qf.at[t + 1], cq)
         hear(2 * t)
         tell(2 * t + 1)
-        for c in range(chunks):
-            arrive(q_halo(t, c))
-            laplace(qf.at[t + 1], qh.at[t], c, use_q)
-            if t < steps - 1:
-                start(q_halo(t + 1, c))
+        arrive(q_halo(t))
+        if t < steps - 1:
+            edges(qf.at[t + 1], cq, qh.at[t], lambda y, at, now, lap: now + move_q(y, at, now, lap), eq.at[t])
+            start(q_halo(t + 1))
+        laplace(qf.at[t + 1], cq, qh.at[t], use_q, *(() if t == steps - 1 else (pf.at[t + 2], cp)))
         hear(2 * t + 1)
         tell(2 * t + 2)
     for i in range(2 * steps, len(reaches) + len(bits)):
@@ -394,7 +423,7 @@
             narrow[j, at, :] = out[j]
         return carry
 
-    lax.fori_loop(0, cx // 8, image, 0, unroll=2)
+    lax.fori_loop(0, cx // 8, image, 0, unroll=4)
     tall = []
     for a in range(pairs):
         high, low = split(jnp.concatenate([narrow[2 * a], narrow[2 * a + 1]], 1))
@@ -447,12 +476,7 @@
     def keep_lap(y, now, lap):
         lap_last[y] = lap
 
-    def last_lap(c):
-        arrive(p_halo(steps, c))
-        laplace(pf.at[steps + 1], ph.at[steps], c, keep_lap)
-
-    for c in range(chunks // 2):
-        last_lap(c)
+    cores(pf.at[steps + 1], cp)
     planes, lines = piece(shot)
     mine = part0[planes, lines, :]
     for d in range(1, n_shot):
@@ -479,11 +503,6 @@
     none = jnp.zeros((group, rows - 2 * OV, 128), F32)
     mine = mine + jnp.concatenate([low_rim, none], 1) + jnp.concatenate([none, high_rim], 1)
     tot[shot] = mine
-    gather = []
-    for d in range(1, n_shot):
-        copy = peer_copy(tot.at[shot], tot.at[shot], d, ag_s, ag_r)
-        copy.start()
-        gather.append(copy)
     squares = jnp.zeros((8, 128), F32)
     first = lax.rem(shot, halfs) * rows
     for g in range(group):
@@ -500,11 +519,16 @@
             },
             device_id_type=MESH,
         ).start()
+    gather = []
+    for d in range(1, n_shot):
+        copy = peer_copy(tot.at[shot], tot.at[shot], d, ag_s, ag_r)
+        copy.start()
+        gather.append(copy)
     last = wave[steps]
     for y in range(cy):
         base[y] = pf[steps + 1, y] + dp[y] + last * src[y]
-    for c in range(chunks // 2, chunks):
-        last_lap(c)
+    arrive(p_halo(steps))
+    laplace(pf.at[steps + 1], cp, ph.at[steps], keep_lap)
     for copy in gather:
         copy.wait()
     left_on = jnp.where(has_left, 1.0, 0.0).astype(F32)
@@ -519,8 +543,8 @@
         ttot[a, OV : OV + cxc, :] = whole[OV : OV + cxc]
         ttot[a, OV + cxc :, :] = whole[OV + cxc :] * right_on
     expand(ttot, exp_t)
-    sent([p_halo(t, c) for t in range(steps + 1) for c in range(chunks)])
-    sent([q_halo(t, c) for t in range(steps) for c in range(chunks)])
+    sent([p_halo(t) for t in range(steps + 1)])
+    sent([q_halo(t) for t in range(steps)])
     others = sq_all.at[pl.ds(1, n_shot * n_tile - 1)]
     everyone = pltpu.make_async_remote_copy(
         src_ref=others, dst_ref=others, send_sem=sq_s, recv_sem=sq_r,
@@ -562,7 +586,7 @@
     ext = cxc + 2 * OV
     group = max(1, pairs // n_shot)
     rows = ext // max(1, n_shot // pairs)
-    dims = (cx, cy, cz, cxc, pairs, steps, group, rows, CHUNKS)
+    dims = (cx, cy, cz, cxc, pairs, steps, group, rows)
     consts = [jnp.asarray(c) for c in constants(cx, cz, cxc, czc)]
     vmem = pl.BlockSpec(memory_space=pltpu.VMEM)
     hbm = pl.BlockSpec(memory_space=pltpu.HBM)
@@ -579,11 +603,12 @@
         scratch_shapes=[
             sem(4), buf(steps + 2, *field), buf(steps + 2, *field), *[buf(*field)] * 2,
             buf(steps, *field), *[buf(*field)] * 5, buf(cyc, cx, cz),
+            *[buf(*field)] * 2, *[buf(steps, 2, cy, OV, cz)] * 2,
             buf(steps + 1, 2, cy, OV, cz), buf(steps, 2, cy, OV, cz),
             buf(pairs, ext, 128), buf(cyc, cx, cz), buf(pairs, ext, 128),
             buf(2, n_shot, group, 2 * OV, 128), buf(max(1, n_shot - 1), group, rows, 128),
             buf(n_shot, group, rows, 128), buf(n_shot * n_tile, 1, 128),
-            *[sem(steps + 1, CHUNKS, 2)] * 2, *[sem(steps, CHUNKS, 2)] * 2,
+            *[sem(steps + 1, 2)] * 2, *[sem(steps, 2)] * 2,
             sem(2), sem(2), sem(2, n_shot), sem(2, n_shot),
             *[sem(max(1, n_shot - 1))] * 4, sem(), sem(),
             pltpu.SemaphoreType.REGULAR((max(1, (n_tile - 2).bit_length()), 2)),

time: 34 us -> 33.2 us (0.976)
  Pallas kernels: 33.2 us -> 32.2 us
    pallas_call x1, Pallas kernels: 32 us -> 31.1 us  [on_device(): pl.pallas_call(functools.partial(kernel, dims, n_shot, n_tile, spline_y),...]
where the time goes in v3:
time: 33.2 us; the launch traced here: 33 us
  Pallas kernels  32.2 us (97%)
  between operations  0.8 us (2%)
    pallas_call x1, Pallas kernels, on_device(): pl.pallas_call(functools.partial(kernel, dims, n_shot, n_tile, spline_y),...  31.1 us
    pallas_call x1, Pallas kernels, on_device(): pl.pallas_call(finish_kernel, out_shape=(like(cxc, merged), like(cx, cy,...  1.17 us

profile of v3, /device:TPU:0, one launch (start us, length us, event | category | flops | bytes accessed | tf_op | source)
XLA Modules:
  0.0 33.0 jit_solution(2494814563351469043)
XLA Ops:
  0.6 31.1 %shard_map.167 = (f32[16,128,128]{2,1,0:T(8,128)S(1)}, f32[16,128,128]{2,1,0:T(8,128)S(1)}, f32[16,128,128]{2,1,0:T(8,128)S(1)}, f32[16,128,128]{2,1,0:T(8,128)S...) custom-call(f32[128,16,128]{2,1,0:T(8,128)} %bitcast.6, f32[128,16,128]{2,1,0:T(8,128)} %bitcast.7, ...), custom_call_target="tpu_custom_call" | custom-call | tf_op jit(solution)/shard_map/pallas_call | solution.py:598
  31.7 1.2 %shard_map.168 = (f32[64,512]{1,0:T(8,128)}, f32[128,16,128]{2,1,0:T(8,128)}) custom-call(f32[16,128,128]{2,1,0:T(8,128)S(1)} %get-tuple-element.10.base, f32[16,128,128]{2,1,0:T(8,128)S(1)} %get-tuple-element.11.lap_last, f32[16,128,128]{2,1,0:T(8,128)S(1)} %get-tuple-element.12.sig, f32[16,128,128]{2,1,0:T(8,128)S(1)} %get-tuple-element.13.exp_t, ...), custom_call_target="tpu_custom_call" | custom-call | tf_op jit(solution)/shard_map/pallas_call | solution.py:627

commit v4 on v3

--- a/solution.py
+++ b/solution.py
@@ -333,7 +333,7 @@
                 out[y, at, :] = functools.reduce(lambda u, v: u + v, terms)
             return carry
 
-        lax.fori_loop(0, cx // 8, body, 0)
+        lax.fori_loop(0, cx // 8, body, 0, unroll=4)
 
     count = elems.shape[1]
     where_to = elems[...]
@@ -348,7 +348,7 @@
         src[y] = lax.dot_general(hits, lanes, (((1,), (1,)), ((), ())), preferred_element_type=F32)
         return carry
 
-    lax.fori_loop(0, cy, source, 0, unroll=2)
+    lax.fori_loop(0, cy, source, 0, unroll=4)
     for copy in small[4:]:
         copy.wait()
     cores(pf.at[1], cp)
@@ -360,7 +360,7 @@
         sig2[y] = value * value
         return carry
 
-    lax.fori_loop(0, cy, square, 0)
+    lax.fori_loop(0, cy, square, 0, unroll=4)
 
     loaded(2)
     loaded(3)
@@ -477,6 +477,8 @@
         lap_last[y] = lap
 
     cores(pf.at[steps + 1], cp)
+    arrive(p_halo(steps))
+    laplace(pf.at[steps + 1], cp, ph.at[steps], keep_lap)
     planes, lines = piece(shot)
     mine = part0[planes, lines, :]
     for d in range(1, n_shot):
@@ -503,6 +505,11 @@
     none = jnp.zeros((group, rows - 2 * OV, 128), F32)
     mine = mine + jnp.concatenate([low_rim, none], 1) + jnp.concatenate([none, high_rim], 1)
     tot[shot] = mine
+    gather = []
+    for d in range(1, n_shot):
+        copy = peer_copy(tot.at[shot], tot.at[shot], d, ag_s, ag_r)
+        copy.start()
+        gather.append(copy)
     squares = jnp.zeros((8, 128), F32)
     first = lax.rem(shot, halfs) * rows
     for g in range(group):
@@ -519,16 +526,9 @@
             },
             device_id_type=MESH,
         ).start()
-    gather = []
-    for d in range(1, n_shot):
-        copy = peer_copy(tot.at[shot], tot.at[shot], d, ag_s, ag_r)
-        copy.start()
-        gather.append(copy)
     last = wave[steps]
     for y in range(cy):
         base[y] = pf[steps + 1, y] + dp[y] + last * src[y]
-    arrive(p_halo(steps))
-    laplace(pf.at[steps + 1], cp, ph.at[steps], keep_lap)
     for copy in gather:
         copy.wait()
     left_on = jnp.where(has_left, 1.0, 0.0).astype(F32)

time: 33.2 us -> 33.1 us (level)
  no operation moved by 1% of the time
where the time goes in v4:
time: 33.1 us; the launch traced here: 32.9 us
  Pallas kernels  32.1 us (97%)
  between operations  0.8 us (2%)
    pallas_call x1, Pallas kernels, on_device(): pl.pallas_call(functools.partial(kernel, dims, n_shot, n_tile, spline_y),...  30.9 us
    pallas_call x1, Pallas kernels, on_device(): pl.pallas_call(finish_kernel, out_shape=(like(cxc, merged), like(cx, cy,...  1.17 us

profile of v4, /device:TPU:0, one launch (start us, length us, event | category | flops | bytes accessed | tf_op | source)
XLA Modules:
  0.0 32.9 jit_solution(3749251606162570313)
XLA Ops:
  0.6 30.9 %shard_map.167 = (f32[16,128,128]{2,1,0:T(8,128)S(1)}, f32[16,128,128]{2,1,0:T(8,128)S(1)}, f32[16,128,128]{2,1,0:T(8,128)S(1)}, f32[16,128,128]{2,1,0:T(8,128)S...) custom-call(f32[128,16,128]{2,1,0:T(8,128)} %bitcast.6, f32[128,16,128]{2,1,0:T(8,128)} %bitcast.7, ...), custom_call_target="tpu_custom_call" | custom-call | tf_op jit(solution)/shard_map/pallas_call | solution.py:598
  31.6 1.2 %shard_map.168 = (f32[64,512]{1,0:T(8,128)}, f32[128,16,128]{2,1,0:T(8,128)}) custom-call(f32[16,128,128]{2,1,0:T(8,128)S(1)} %get-tuple-element.10.base, f32[16,128,128]{2,1,0:T(8,128)S(1)} %get-tuple-element.11.lap_last, f32[16,128,128]{2,1,0:T(8,128)S(1)} %get-tuple-element.12.sig, f32[16,128,128]{2,1,0:T(8,128)S(1)} %get-tuple-element.13.exp_t, ...), custom_call_target="tpu_custom_call" | custom-call | tf_op jit(solution)/shard_map/pallas_call | solution.py:627
